TPU v7x, 32 devices: a whole 2x2x4 slice. The times are simulated.
32 devices in a mesh: case: 2 (over x), ax: 16 (over z, y, core).
Axes of the slice: x: 2, y: 2, z: 4, core: 2. Of those that a mesh axis runs over, the one named last changes fastest.
Arguments:
- populations: float32 [19, 32, 128, 128], P(None, 'ax', 'case'), parts along dimension 2, may hold values from 0 to 1, as said below
- solid_mask: int32 [32, 128, 128], P('ax', 'case'), parts along dimension 1, may hold values from 0 to 1, as said below
- link_flags: int32 [2, 32, 128, 128], P(None, 'ax', 'case'), parts along dimension 2, may hold values from 0 to 511, as said below
- inlet_cells: int32 [1024], P('case'), parts along dimension 0, may hold values from 0 to 8191, as said below
- pod_basis: float32 [512, 3, 512], P(None, None, 'ax'), may hold values from -0.15625 to 0.15625
- mri_frames: float32 [24, 6, 512], P(None, 'case', 'ax'), parts along dimension 1
- frame_index: int32 [1], replicated, may hold values from 0 to 23
Outputs:
- advanced_populations: float32 [19, 32, 128, 128], P(None, 'ax', 'case'), parts along dimension 2
- inflow: float32 [2, 6, 512], P(None, 'case', 'ax'), parts along dimension 1
There are 2 independent parts, one for each index of `case`. A program takes and returns all parts, laid end to end along the dimension named above; an argument that names none is the same for every part. Nothing has to cross between parts.
Inputs may be any that keep to these rules, and one draw needn't show every extreme that they name: `solid_mask`: 1 marks a wall cell, 0 a fluid cell; the two outermost rows and columns of every cross-section are wall cells. `link_flags`: at a fluid cell, bit (i - 1) mod 9 of word (i - 1) div 9 is set exactly when the cell at minus c_i is a wall cell, the grid being continued past its first and last plane by repeating those planes; zero at wall cells. `inlet_cells`: distinct cells of the first plane, all of them fluid cells. `populations`: every entry is positive.
All inputs are finite; a program needn't handle non-finite values.
Results may differ from a plain program's by a relative error of at most 0.00011.
Values sent between devices are 32-bit elements; how exact they have to be, the bound alone decides.
A program may use at most 64 MiB of HBM per device.

v0:
```python
import math

import jax
import jax.numpy as jnp
from jax import lax
from jax.sharding import PartitionSpec as P

STEPS = 2


lattice_c = (
    (0, 0, 0),
    (1, 0, 0),
    (-1, 0, 0),
    (0, 1, 0),
    (0, -1, 0),
    (0, 0, 1),
    (0, 0, -1),
    (1, 1, 0),
    (-1, -1, 0),
    (1, -1, 0),
    (-1, 1, 0),
    (1, 0, 1),
    (-1, 0, -1),
    (1, 0, -1),
    (-1, 0, 1),
    (0, 1, 1),
    (0, -1, -1),
    (0, 1, -1),
    (0, -1, 1),
)
lattice_w = (1.0 / 3.0,) + (1.0 / 18.0,) * 6 + (1.0 / 36.0,) * 12
opposite_of = (0, 2, 1, 4, 3, 6, 5, 8, 7, 10, 9, 12, 11, 14, 13, 16, 15, 18, 17)
pair_list = ((0, 0), (1, 1), (2, 2), (0, 1), (0, 2), (1, 2))
relax_base = 0.52
smagorinsky_sq = 0.04
inflow_scale = 0.05


def extended(array, sides, width):
    for axis, dim in sides:
        count, length = (lax.axis_size(axis), array.shape[dim])
        up = [(i, (i + 1) % count) for i in range(count - 1)]
        down = [(j, i) for i, j in up]
        last = lax.slice_in_dim(array, length - width, length, axis=dim)
        leading = lax.slice_in_dim(array, 0, width, axis=dim)
        before = lax.ppermute(last, axis, up)
        after = lax.ppermute(leading, axis, down)
        array = jnp.concatenate([before, array, after], axis=dim)
    return array


def moment_rows():
    listed = [[1.0] * 19]
    for axis_a in range(3):
        listed.append([float(vector[axis_a]) for vector in lattice_c])
    for pair_a, pair_b in pair_list:
        listed.append([float(vector[pair_a] * vector[pair_b]) for vector in lattice_c])
    return jnp.asarray(listed, dtype=jnp.float32)


def equilibrium(density, velocity):
    lattice = jnp.asarray(
        [[float(entry) for entry in vector] for vector in lattice_c], dtype=jnp.float32
    )
    weights = jnp.asarray(list(lattice_w), dtype=jnp.float32).reshape((19,) + (1,) * density.ndim)
    projected = jnp.einsum("iq,q...->i...", lattice, velocity, precision=lax.Precision.HIGHEST)
    speed_sq = jnp.sum(velocity * velocity, axis=0)
    return (
        weights
        * density[None]
        * (1.0 + 3.0 * projected + 4.5 * projected * projected - 1.5 * speed_sq[None])
    )


def collide(populations, solid_mask):
    moments = jnp.einsum(
        "mi,i...->m...", moment_rows(), populations, precision=lax.Precision.HIGHEST
    )
    density = moments[0]
    velocity = moments[1:4] / density[None]
    nonequil = populations - equilibrium(density, velocity)
    stress = jnp.einsum(
        "mi,i...->m...", moment_rows()[4:], nonequil, precision=lax.Precision.HIGHEST
    )
    magnitude = stress[0] * stress[0] + stress[1] * stress[1] + stress[2] * stress[2]
    magnitude = magnitude + 2.0 * (
        stress[3] * stress[3] + stress[4] * stress[4] + stress[5] * stress[5]
    )
    relax_time = 0.5 * (
        relax_base
        + jnp.sqrt(
            relax_base * relax_base
            + 18.0 * math.sqrt(2.0) * smagorinsky_sq * jnp.sqrt(magnitude) / density
        )
    )
    relaxed = populations - nonequil / relax_time[None]
    return jnp.where(solid_mask[None] == 1, populations, relaxed)


def stream(relaxed, ghost_low, ghost_high, link_flags, solid_mask):
    padded = jnp.concatenate([ghost_low[:, None], relaxed, ghost_high[:, None]], axis=1)
    planes_here = relaxed.shape[1]
    read = []
    for direction in range(19):
        step_x, step_y, step_z = lattice_c[direction]
        source = padded[direction, 1 - step_z : 1 - step_z + planes_here]
        source = jnp.roll(source, (step_y, step_x), axis=(1, 2))
        if direction > 0:
            word = link_flags[(direction - 1) // 9]
            linked = jnp.bitwise_and(jnp.right_shift(word, (direction - 1) % 9), 1)
            source = jnp.where(linked == 1, relaxed[opposite_of[direction]], source)
        read.append(jnp.where(solid_mask == 1, relaxed[direction], source))
    return jnp.stack(read)


def inlet_plane(speeds, inlet_cells, height, plane_width):
    inlet_speed = jnp.zeros((3, height * plane_width), jnp.float32).at[:, inlet_cells].set(speeds)
    inlet_speed = inlet_speed.reshape(3, height, plane_width)
    return equilibrium(jnp.ones((height, plane_width), jnp.float32), inlet_speed)


def neighbour_planes(relaxed):
    padded = extended(relaxed, (("ax", 1),), 1)
    ghost_low = padded[:, 0]
    ghost_high = padded[:, -1]
    return (ghost_low, ghost_high)


def body(populations, solid_mask, link_flags, inlet_cells, pod_basis, mri_frames, frame_index):
    frames_total = mri_frames.shape[0]
    frame_slot = lax.broadcasted_iota(jnp.int32, (STEPS, frames_total), 1)
    segment_slot = lax.broadcasted_iota(jnp.int32, (STEPS, frames_total), 0)
    selector = (frame_slot == (frame_index[0] + segment_slot) % frames_total).astype(jnp.float32)
    chosen = jnp.einsum("sf,fjc->sjc", selector, mri_frames, precision=lax.Precision.HIGHEST)
    partial_terms = jnp.einsum("kjc,sjc->sk", pod_basis, chosen, precision=lax.Precision.HIGHEST)
    coefficients = lax.psum(partial_terms, "ax")
    local_inflow = jnp.einsum(
        "kjc,sk->sjc", pod_basis, coefficients, precision=lax.Precision.HIGHEST
    )
    whole_inflow = lax.all_gather(local_inflow, "ax", axis=2, tiled=True)
    position = lax.axis_index("ax")
    axis_count = lax.axis_size("ax")
    height = populations.shape[2]
    plane_width = populations.shape[3]
    for segment_index in range(STEPS):
        relaxed = collide(populations, solid_mask)
        inlet_ghost = inlet_plane(
            inflow_scale * whole_inflow[segment_index], inlet_cells, height, plane_width
        )
        ghost_low, ghost_high = neighbour_planes(relaxed)
        ghost_low = jnp.where(position == 0, inlet_ghost, ghost_low)
        ghost_high = jnp.where(position == axis_count - 1, relaxed[:, -1], ghost_high)
        populations = stream(relaxed, ghost_low, ghost_high, link_flags, solid_mask)
    return (populations, local_inflow)


def solution(mesh):
    in_specs = (
        P(None, "ax", "case", None),
        P("ax", "case", None),
        P(None, "ax", "case", None),
        P("case"),
        P(None, None, "ax"),
        P(None, "case", "ax"),
        P(),
    )
    out_specs = (P(None, "ax", "case", None), P(None, "case", "ax"))
    return jax.shard_map(body, mesh=mesh, in_specs=in_specs, out_specs=out_specs, check_vma=False)
```

profile of v0, /device:TPU:1, one launch (start us, length us, event | category | flops | bytes accessed | tf_op | source)
XLA Modules:
  0.0 146.1 jit_solution(2449302820524212767)
XLA Ops:
  0.6 0.9 broadcast_compare_fusion
  1.6 3.0 %fusion.4 = f32[10,2,64,128]{3,0,2,1:T(8,128)S(1)} fusion(f32[10,19,1,1]{1,0,3,2:T(8,128)} %constant.81, f32[19,2,64,128]{3,2,1,0:T(8,128)} %param.19), kind=kOutput, calls=%fused_computation.12 | convolution fusion | flops 37355520 | bytes 1901304 | tf_op jit(solution)/shard_map/mi,i...->m.../dot_general | solution.py:77
  4.6 0.2 multiply_reduce_fusion.3
  4.9 1.5 %fusion.149 = f32[19,2,64,128]{3,0,2,1:T(8,128)S(1)} fusion(f32[19,3,1,1]{0,1,3,2:T(4,128)S(1)} %copy-done.22, f32[10,2,64,128]{3,0,2,1:T(8,128)S(1)} %fusion.4, f32[2,64,128]{2,1,0:T(8,128)S(1)} %bitcast.600), kind=kOutput, calls=%fused_computation.338 | convolution fusion | flops 11255808 | bytes 1574912 | tf_op jit(solution)/shard_map/iq,q...->i.../dot_general | solution.py:67
  6.4 0.4 copy_multiply_fusion.2
  6.8 0.8 copy-done.3
  7.7 2.8 %copy_subtract_fusion = f32[19,2,64,128]{3,0,2,1:T(8,128)S(1)} fusion(f32[19,2,64,128]{3,2,1,0:T(8,128)S(1)} %copy-done.3, f32[19,2,64,128]{3,2,1,0:T(8,128)S(1)} %get-tuple-element.100, f32[19,2,64,128]{3,2,1,0:T(8,128)S(1)} %get-tuple-element.61, f32[19,2,64,128]{3,0,2,1:T(8,128)S(1)} %fusion.149, f32[19,2,64,128]{3,2,1,0:T(8,128)S(1)} %get-tuple-element.60, ...), kind=kLoop, calls=%fused_computation.11 | loop fusion | flops 1556480 | bytes 7536640 | tf_op jit(solution)/shard_map/sub | solution.py:82
  10.5 0.9 fusion.171
  11.5 0.3 fusion.170
  11.9 1.0 subtract_select_fusion
  12.8 0.2 copy.143
  13.1 0.9 copy-done.5
  14.1 2.1 %collective-permute-start.1 = (f32[19,1,64,128]{3,2,1,0:T(8,128)S(1)}, f32[19,1,64,128]{3,2,1,0:T(8,128)}, u32[]{:S(2)}, u32[]{:S(2)}) collective-permute-start(f32[19,1,64,128]{3,2,1,0:T(8,128)S(1)} %slice.827), channel_id=1, source_target_pairs={{1,0},{2,1},{3,2},{4,3},{5,4},{6,5},{7,6},{8,7},{9,8},{10,9},{11,1... | collective-permute-start | bytes 1867784 | tf_op jit(solution)/shard_map/ppermute | solution.py:48
  16.1 0.6 slice_bitcast_fusion.36
  17.5 0.2 fusion.141
  17.7 0.3 convolution_bitcast_fusion
  18.0 31.4 %psum.7 = f32[2,512]{1,0:T(2,128)S(1)} all-reduce(f32[2,512]{1,0:T(2,128)S(1)} %convolution_bitcast_fusion), channel_id=1, replica_groups=mesh['case'=2,'ax'=16] {'ax'}, use_global_device_ids=true, to_apply=%region_1.2 | all-reduce | flops 1024 | bytes 8192 | tf_op jit(solution)/shard_map/psum | solution.py:137
  49.3 1.0 fusion.139
  50.4 0.5 compare_select_fusion
  50.9 0.8 copy.150
  51.7 23.9 %all_gather.3 = f32[2,3,512]{1,0,2:T(2,128)S(1)} all-gather(f32[2,3,32]{1,0,2:T(2,128)S(1)} %copy.150), channel_id=1, replica_groups=mesh['case'=2,'ax'=16] {'ax'}, dimensions={2}, use_global_device_ids=true | all-gather | bytes 13056 | tf_op jit(solution)/shard_map/all_gather | solution.py:141
  75.6 1.4 slice_multiply_fusion
  77.1 0.6 constant_dynamic-update-slice_fusion.17
  77.7 0.6 copy-done.9
  78.3 0.7 slice.815
  79.0 4.3 %scatter_custom_fusion = f32[3,8192]{0,1:T(8,128)} fusion(s32[512]{0:T(512)} %compare_select_fusion, f32[512,3]{1,0:T(8,128)} %bitcast.636, f32[]{:T(128)} %constant.31.clone.1), kind=kCustom, calls=%fused_computation.7 | custom fusion | bytes 98816 | tf_op jit(solution)/shard_map/scatter | solution.py:118
  83.4 3.4 %multiply_reduce_fusion.1 = f32[8192]{0:T(1024)S(1)} fusion(f32[3,8192]{0,1:T(8,128)} %scatter_custom_fusion), kind=kLoop, calls=%fused_computation.3 | loop fusion | flops 40960 | bytes 131072 | tf_op jit(solution)/shard_map/reduce_sum | solution.py:68
  86.7 0.6 constant_dynamic-update-slice_fusion.16
  87.4 0.6 constant_dynamic-update-slice_fusion.15
  88.0 0.6 multiply_bitcast_fusion.3
  88.6 4.3 %scatter_custom_fusion.1 = f32[3,8192]{0,1:T(8,128)} fusion(s32[512]{0:T(512)} %compare_select_fusion, f32[512,3]{1,0:T(8,128)} %bitcast.635, f32[]{:T(128)} %constant.31.clone.1), kind=kCustom, calls=%fused_computation.5 | custom fusion | bytes 98816 | tf_op jit(solution)/shard_map/scatter | solution.py:118
  92.9 3.5 %multiply_reduce_fusion = f32[8192]{0:T(1024)S(1)} fusion(f32[3,8192]{0,1:T(8,128)} %scatter_custom_fusion.1), kind=kLoop, calls=%fused_computation.2 | loop fusion | flops 40960 | bytes 131072 | tf_op jit(solution)/shard_map/reduce_sum | solution.py:68
  96.4 4.6 %fusion.172 = f32[19,64,128]{2,0,1:T(8,128)} fusion(f32[19,3,1]{0,1,2:T(4,128)S(1)} %copy-done.24, f32[3,64,128]{0,2,1:T(8,128)S(1)} %bitcast.598), kind=kOutput, calls=%fused_computation.343 | convolution fusion | flops 5603328 | bytes 721124 | tf_op jit(solution)/shard_map/iq,q...->i.../dot_general | solution.py:67
  101.0 2.0 %bitcast_select_fusion = (f32[19,1,64,128]{3,2,1,0:T(8,128)S(1)}, f32[19,1,64,128]{3,2,1,0:T(8,128)}) fusion(f32[19,1,64,128]{3,2,1,0:T(8,128)} %collective-permute-done.1, pred[]{:T(512)S(6)} %eq.197, f32[19,2,64,128]{3,2,1,0:T(8,128)S(1)} %copy.143), kind=kLoop, calls=%fused_computation.45 | loop fusion | flops 155648 | bytes 2490369 | tf_op jit(solution)/shard_map/jit(_where)/select_n | solution.py:153
  103.1 3.9 %collective-permute-start = (f32[19,1,64,128]{3,2,1,0:T(8,128)}, f32[19,1,64,128]{3,2,1,0:T(8,128)}, u32[]{:S(2)}, u32[]{:S(2)}) collective-permute-start(f32[19,1,64,128]{3,2,1,0:T(8,128)} %get-tuple-element.80), channel_id=1, source_target_pairs={{0,1},{1,2},{2,3},{3,4},{4,5},{5,6},{6,7},{7,8},{8,9},{9,10},{10,1... | collective-permute-start | bytes 1867784 | tf_op jit(solution)/shard_map/ppermute | solution.py:47
  107.0 1.7 %slice.867 = f32[1,2,64,128]{3,0,2,1:T(1,128)} slice(f32[19,2,64,128]{3,0,2,1:T(8,128)} %copy-done.5), slice={[18:19], [0:2], [0:64], [0:128]} | slice | bytes 131072 | tf_op jit(solution)/shard_map/slice | solution.py:112
  108.8 0.6 slice.822
  109.3 0.6 slice.821
  110.0 0.9 constant_dynamic-update-slice_fusion.14
  110.9 5.6 %fusion.173 = f32[19,64,128]{2,0,1:T(8,128)S(1)} fusion(f32[19,3,1]{0,1,2:T(4,128)} %constant.84, f32[3,64,128]{0,2,1:T(8,128)} %bitcast.597), kind=kOutput, calls=%fused_computation.344 | convolution fusion | flops 5603328 | bytes 721124 | tf_op jit(solution)/shard_map/iq,q...->i.../dot_general | solution.py:67
  116.5 1.3 fusion.19
  118.4 0.1 slice_maximum_fusion.7
  118.7 0.1 constant_dynamic-update-slice_fusion.10
  118.9 0.1 constant_dynamic-update-slice_fusion.9
  119.2 0.1 constant_dynamic-update-slice_fusion.7
  119.3 0.1 constant_dynamic-update-slice_fusion.6
  119.4 0.1 constant_dynamic-update-slice_fusion.5
  119.6 0.4 copy-done.7
  120.2 1.7 %fusion.8 = f32[10,2,64,128]{3,0,2,1:T(8,128)S(1)} fusion(f32[10,19,1,1]{1,0,3,2:T(8,128)S(1)} %copy-done.19, f32[19,2,64,128]{3,2,1,0:T(8,128)S(1)} %get-tuple-element.2), kind=kOutput, calls=%fused_computation.16 | convolution fusion | flops 37355520 | bytes 1901304 | tf_op jit(solution)/shard_map/mi,i...->m.../dot_general | solution.py:77
  121.9 0.2 multiply_reduce_fusion.2
  122.2 1.5 %fusion.150 = f32[19,2,64,128]{3,0,2,1:T(8,128)S(1)} fusion(f32[19,3,1,1]{0,1,3,2:T(4,128)S(1)} %copy-done.23, f32[10,2,64,128]{3,0,2,1:T(8,128)S(1)} %fusion.8, f32[2,64,128]{2,1,0:T(8,128)S(1)} %bitcast.604), kind=kOutput, calls=%fused_computation.339 | convolution fusion | flops 11255808 | bytes 1574912 | tf_op jit(solution)/shard_map/iq,q...->i.../dot_general | solution.py:67
  123.7 0.4 fusion.14
  124.2 0.2 copy-done.21
  124.4 1.6 %fusion.6 = f32[6,2,64,128]{3,0,2,1:T(8,128)S(1)} fusion(f32[6,19,1,1]{1,0,3,2:T(8,128)S(1)} %copy-done.21, f32[19,2,64,128]{3,2,1,0:T(8,128)S(1)} %fusion.14), kind=kOutput, calls=%fused_computation.14 | convolution fusion | flops 22413312 | bytes 1638856 | tf_op jit(solution)/shard_map/mi,i...->m.../dot_general | solution.py:83
  126.0 0.3 fusion.169
  126.4 0.3 subtract_select_fusion.1
  126.8 2.3 %collective-permute-start.2 = (f32[19,1,64,128]{3,2,0,1:T(8,128)S(1)}, f32[19,1,64,128]{3,2,0,1:T(8,128)S(1)}, u32[]{:S(2)}, u32[]{:S(2)}) collective-permute-start(f32[19,1,64,128]{3,2,0,1:T(8,128)S(1)} %get-tuple-element.67), channel_id=1, source_target_pairs={{0,1},{1,2},{2,3},{3,4},{4,5},{5,6},{6,7},{7,8},{8,9},{9,10},{10,1... | collective-permute-start | bytes 1867784 | tf_op jit(solution)/shard_map/ppermute | solution.py:47
  129.2 0.1 slice_bitcast_fusion.17
  129.6 2.1 %collective-permute-start.3 = (f32[19,1,64,128]{3,2,0,1:T(8,128)S(1)}, f32[19,1,64,128]{3,2,0,1:T(8,128)S(1)}, u32[]{:S(2)}, u32[]{:S(2)}) collective-permute-start(f32[19,1,64,128]{3,2,0,1:T(8,128)S(1)} %get-tuple-element.66), channel_id=1, source_target_pairs={{1,0},{2,1},{3,2},{4,3},{5,4},{6,5},{7,6},{8,7},{9,8},{10,9},{11,1... | collective-permute-start | bytes 1867784 | tf_op jit(solution)/shard_map/ppermute | solution.py:48
  131.7 11.2 %collective-permute-done.2 = f32[19,1,64,128]{3,2,0,1:T(8,128)S(1)} collective-permute-done((f32[19,1,64,128]{3,2,0,1:T(8,128)S(1)}, f32[19,1,64,128]{3,2,0,1:T(8,128)S(1)}, u32[]{:S(2)}, u32[]{:S(2)}) %collective-permute-start.2) | collective-permute-done | bytes 622624 | tf_op jit(solution)/shard_map/ppermute | solution.py:47
  142.9 0.2 fusion.24
  143.8 0.1 slice_maximum_fusion.3
  144.1 0.1 slice_maximum_fusion
  145.1 1.0 copy-done.27
  (140 shorter events, 3.7 us)
Async XLA Ops:
  0.6 17.1 %copy-start = (f32[512,3,32]{0,2,1:T(8,128)S(1)}, f32[512,3,32]{0,2,1:T(8,128)}, u32[]{:S(2)}) copy-start(f32[512,3,32]{0,2,1:T(8,128)} %param.23) | copy-start | bytes 589828
  1.5 3.3 %copy-start.22 = (f32[19,3,1,1]{0,1,3,2:T(4,128)S(1)}, f32[19,3,1,1]{0,1,3,2:T(4,128)}, u32[]{:S(2)}) copy-start(f32[19,3,1,1]{0,1,3,2:T(4,128)} %constant.82) | copy-start | bytes 688
  4.8 1.5 %copy-start.25 = (f32[19]{0:T(128)S(1)}, f32[19]{0:T(128)}, u32[]{:S(2)}) copy-start(f32[19]{0:T(128)} %constant.24.clone) | copy-start | bytes 232
  6.4 1.3 copy-start.3
  7.7 2.8 %copy-start.20 = (f32[6,19,1,1]{1,0,3,2:T(8,128)S(1)}, f32[6,19,1,1]{1,0,3,2:T(8,128)}, u32[]{:S(2)}) copy-start(f32[6,19,1,1]{1,0,3,2:T(8,128)} %constant.83) | copy-start | bytes 1372
  12.8 1.2 copy-start.5
  14.0 3.5 %copy-start.29 = (f32[24,3,32]{2,0,1:T(8,128)S(1)}, f32[24,3,32]{2,0,1:T(8,128)}, u32[]{:S(2)}) copy-start(f32[24,3,32]{2,0,1:T(8,128)} %param.24) | copy-start | bytes 27652
  14.0 36.4 %copy-start.28 = (s32[512]{0:T(512)S(1)}, s32[512]{0:T(512)}, u32[]{:S(2)}) copy-start(s32[512]{0:T(512)} %param.22) | copy-start | bytes 6148
  14.1 87.0 %collective-permute-start.1 = (f32[19,1,64,128]{3,2,1,0:T(8,128)S(1)}, f32[19,1,64,128]{3,2,1,0:T(8,128)}, u32[]{:S(2)}, u32[]{:S(2)}) collective-permute-start(f32[19,1,64,128]{3,2,1,0:T(8,128)S(1)} %slice.827), channel_id=1, source_target_pairs={{1,0},{2,1},{3,2},{4,3},{5,4},{6,5},{7,6},{8,7},{9,8},{10,9},{11,1... | collective-permute-start | bytes 1867784 | tf_op jit(solution)/shard_map/ppermute | solution.py:48
  16.8 60.3 %copy-start.1 = (s32[2,64,128]{2,1,0:T(8,128)S(1)}, s32[2,64,128]{2,1,0:T(8,128)}, u32[]{:S(2)}) copy-start(s32[2,64,128]{2,1,0:T(8,128)} %param.20) | copy-start | bytes 196612
  16.8 60.3 %copy-start.4 = (s32[2,2,64,128]{3,2,1,0:T(8,128)S(1)}, s32[2,2,64,128]{3,2,1,0:T(8,128)}, u32[]{:S(2)}) copy-start(s32[2,2,64,128]{3,2,1,0:T(8,128)} %param.21) | copy-start | bytes 393220
  51.7 25.3 %copy-start.8 = (f32[2,64,128]{2,1,0:T(8,128)S(1)}, f32[2,64,128]{2,1,0:T(8,128)}, u32[]{:S(2)}) copy-start(f32[2,64,128]{2,1,0:T(8,128)} %get-tuple-element.84) | copy-start | bytes 196612
  77.7 0.6 copy-start.9
  77.7 1.3 copy-start.12
  83.3 3.4 %copy-start.10 = (f32[2,64,128]{2,1,0:T(8,128)S(1)}, f32[2,64,128]{2,1,0:T(8,128)}, u32[]{:S(2)}) copy-start(f32[2,64,128]{2,1,0:T(8,128)} %copy-done.9) | copy-start | bytes 196612
  83.3 3.4 %copy-start.14 = (f32[2,64,127]{2,1,0:T(8,128)S(1)}, f32[2,64,127]{2,1,0:T(8,128)}, u32[]{:S(2)}) copy-start(f32[2,64,127]{2,1,0:T(8,128)} %slice.815) | copy-start | bytes 195076
  83.3 4.0 %copy-start.13 = (f32[2,64,128]{2,1,0:T(8,128)S(1)}, f32[2,64,128]{2,1,0:T(8,128)}, u32[]{:S(2)}) copy-start(f32[2,64,128]{2,1,0:T(8,128)} %copy-done.12) | copy-start | bytes 196612
  92.9 3.5 %copy-start.2 = (f32[3,8192]{0,1:T(8,128)S(1)}, f32[3,8192]{0,1:T(8,128)}, u32[]{:S(2)}) copy-start(f32[3,8192]{0,1:T(8,128)} %scatter_custom_fusion) | copy-start | bytes 294916
  92.9 3.5 %copy-start.24 = (f32[19,3,1]{0,1,2:T(4,128)S(1)}, f32[19,3,1]{0,1,2:T(4,128)}, u32[]{:S(2)}) copy-start(f32[19,3,1]{0,1,2:T(4,128)} %constant.84) | copy-start | bytes 688
  101.0 7.7 %copy-start.11 = (f32[2,64,128]{2,1,0:T(8,128)S(1)}, f32[2,64,128]{2,1,0:T(8,128)}, u32[]{:S(2)}) copy-start(f32[2,64,128]{2,1,0:T(8,128)} %get-tuple-element.81) | copy-start | bytes 196612
  103.1 13.4 %collective-permute-start = (f32[19,1,64,128]{3,2,1,0:T(8,128)}, f32[19,1,64,128]{3,2,1,0:T(8,128)}, u32[]{:S(2)}, u32[]{:S(2)}) collective-permute-start(f32[19,1,64,128]{3,2,1,0:T(8,128)} %get-tuple-element.80), channel_id=1, source_target_pairs={{0,1},{1,2},{2,3},{3,4},{4,5},{5,6},{6,7},{7,8},{8,9},{9,10},{10,1... | collective-permute-start | bytes 1867784 | tf_op jit(solution)/shard_map/ppermute | solution.py:47
  110.9 5.6 %copy-start.6 = (f32[19,64,128]{2,0,1:T(8,128)S(1)}, f32[19,64,128]{2,0,1:T(8,128)}, u32[]{:S(2)}) copy-start(f32[19,64,128]{2,0,1:T(8,128)} %fusion.172) | copy-start | bytes 1867780
  110.9 5.6 %copy-start.15 = (f32[64,128]{1,0:T(8,128)S(1)}, f32[64,128]{1,0:T(8,128)}, u32[]{:S(2)}) copy-start(f32[64,128]{1,0:T(8,128)} %multiply_bitcast_fusion.3) | copy-start | bytes 98308
  110.9 5.6 %copy-start.26 = (f32[19]{0:T(128)S(1)}, f32[19]{0:T(128)}, u32[]{:S(2)}) copy-start(f32[19]{0:T(128)} %constant.24.clone) | copy-start | bytes 232
  119.2 0.8 copy-start.7
  119.4 0.8 copy-start.19
  120.2 2.0 %copy-start.23 = (f32[19,3,1,1]{0,1,3,2:T(4,128)S(1)}, f32[19,3,1,1]{0,1,3,2:T(4,128)}, u32[]{:S(2)}) copy-start(f32[19,3,1,1]{0,1,3,2:T(4,128)} %constant.82) | copy-start | bytes 688
  123.7 0.7 copy-start.21
  126.7 2.5 %copy-start.16 = (pred[2,64,128]{2,1,0:T(8,128)(4,1)S(1)}, pred[2,64,128]{2,1,0:T(8,128)(4,1)}, u32[]{:S(2)}) copy-start(pred[2,64,128]{2,1,0:T(8,128)(4,1)} %get-tuple-element.37) | copy-start | bytes 49156
  126.7 2.7 %copy-start.18 = (pred[2,64,128]{2,1,0:T(8,128)(4,1)S(1)}, pred[2,64,128]{2,1,0:T(8,128)(4,1)}, u32[]{:S(2)}) copy-start(pred[2,64,128]{2,1,0:T(8,128)(4,1)} %get-tuple-element.35) | copy-start | bytes 49156
  126.8 2.7 %copy-start.17 = (pred[2,64,128]{2,1,0:T(8,128)(4,1)S(1)}, pred[2,64,128]{2,1,0:T(8,128)(4,1)}, u32[]{:S(2)}) copy-start(pred[2,64,128]{2,1,0:T(8,128)(4,1)} %get-tuple-element.33) | copy-start | bytes 49156
  126.8 16.1 %collective-permute-start.2 = (f32[19,1,64,128]{3,2,0,1:T(8,128)S(1)}, f32[19,1,64,128]{3,2,0,1:T(8,128)S(1)}, u32[]{:S(2)}, u32[]{:S(2)}) collective-permute-start(f32[19,1,64,128]{3,2,0,1:T(8,128)S(1)} %get-tuple-element.67), channel_id=1, source_target_pairs={{0,1},{1,2},{2,3},{3,4},{4,5},{5,6},{6,7},{7,8},{8,9},{9,10},{10,1... | collective-permute-start | bytes 1867784 | tf_op jit(solution)/shard_map/ppermute | solution.py:47
  129.6 13.7 %collective-permute-start.3 = (f32[19,1,64,128]{3,2,0,1:T(8,128)S(1)}, f32[19,1,64,128]{3,2,0,1:T(8,128)S(1)}, u32[]{:S(2)}, u32[]{:S(2)}) collective-permute-start(f32[19,1,64,128]{3,2,0,1:T(8,128)S(1)} %get-tuple-element.66), channel_id=1, source_target_pairs={{1,0},{2,1},{3,2},{4,3},{5,4},{6,5},{7,6},{8,7},{9,8},{10,9},{11,1... | collective-permute-start | bytes 1867784 | tf_op jit(solution)/shard_map/ppermute | solution.py:48
  145.1 1.0 copy-start.27
where the time goes:
time: 147 us; the launch traced here: 146 us
  blocking collectives  55.3 us (38%)
  other arithmetic  25.1 us (17%)
  matrix products  21.8 us (15%)
  local copies, waits for them, and re-layouts  20 us (14%)
  waiting for transfers between devices  11.2 us (8%)
  starting transfers between devices  10.4 us (7%)
  between operations  2.29 us (2%)
    psum x1, blocking collectives, body(): coefficients = lax.psum(partial_terms, 'ax')  31.4 us
    all_gather x1, blocking collectives, body(): whole_inflow = lax.all_gather(local_inflow, 'ax', axis=2, tiled=True)  23.9 us
    dot_general x4, matrix products, equilibrium(): jnp.einsum('iq,q...->i...', lattice, velocity, precision=lax.Precision.HI...  13.1 us
    ppermute x2, waiting for transfers between devices, extended(): before = lax.ppermute(last, axis, up)  11.2 us
    scatter x2, local copies, waits for them, and re-layouts, inlet_plane(): jnp.zeros((3, height * plane_width), jnp.float32).at[:, inlet_cells]  8.61 us
    reduce_sum x4, other arithmetic, equilibrium(): speed_sq = jnp.sum(velocity * velocity, axis=0)  7.34 us
    ppermute x2, starting transfers between devices, extended(): before = lax.ppermute(last, axis, up)  6.2 us
    dot_general x2, matrix products, collide(): jnp.einsum('mi,i...->m...', moment_rows(), populations, precision=lax.Pre...  4.7 us
  transfers between devices with their start and end apart: 4, of which 1 were waited for; matrix products, arithmetic and copies ran while one was open for 26% of the time, Pallas kernels for 0%

commit v1 on v0

v1 whole, which is shorter than its diff:
```python
import functools
import math

import jax
import jax.numpy as jnp
from jax import lax
from jax.experimental import pallas as pl
from jax.experimental.pallas import tpu as pltpu
from jax.sharding import PartitionSpec as P

STEPS = 2
MESH = pl.DeviceIdType.MESH
HIGHEST = lax.Precision.HIGHEST
PAD = 8
LANES = 128

lattice_c = (
    (0, 0, 0),
    (1, 0, 0),
    (-1, 0, 0),
    (0, 1, 0),
    (0, -1, 0),
    (0, 0, 1),
    (0, 0, -1),
    (1, 1, 0),
    (-1, -1, 0),
    (1, -1, 0),
    (-1, 1, 0),
    (1, 0, 1),
    (-1, 0, -1),
    (1, 0, -1),
    (-1, 0, 1),
    (0, 1, 1),
    (0, -1, -1),
    (0, 1, -1),
    (0, -1, 1),
)
lattice_w = (1.0 / 3.0,) + (1.0 / 18.0,) * 6 + (1.0 / 36.0,) * 12
opposite_of = (0, 2, 1, 4, 3, 6, 5, 8, 7, 10, 9, 12, 11, 14, 13, 16, 15, 18, 17)
relax_base = 0.52
smagorinsky_sq = 0.04
inflow_scale = 0.05

up_dirs = tuple(i for i in range(19) if lattice_c[i][2] == 1)
down_dirs = tuple(i for i in range(19) if lattice_c[i][2] == -1)
flat_dirs = tuple(i for i in range(19) if lattice_c[i][2] == 0)
slot_of = {d: k for k, d in enumerate(up_dirs + down_dirs + flat_dirs)}
CROSS = len(up_dirs)


def relax(f, solid):
    pair = [f[i] + f[i + 1] for i in range(1, 19, 2)]
    diff = [f[i] - f[i + 1] for i in range(1, 19, 2)]
    in_xy = pair[3] + pair[4]
    in_xz = pair[5] + pair[6]
    in_yz = pair[7] + pair[8]
    density = (f[0] + pair[0]) + (pair[1] + pair[2]) + (in_xy + in_xz) + in_yz
    flux = (
        diff[0] + (diff[3] + diff[4]) + (diff[5] + diff[6]),
        diff[1] + (diff[3] - diff[4]) + (diff[7] + diff[8]),
        diff[2] + (diff[5] - diff[6]) + (diff[7] - diff[8]),
    )
    inverse = 1.0 / density
    speed = [j * inverse for j in flux]
    third = density * (1.0 / 3.0)
    square = [j * u for j, u in zip(flux, speed)]
    s_xx = pair[0] + in_xy + in_xz - third - square[0]
    s_yy = pair[1] + in_xy + in_yz - third - square[1]
    s_zz = pair[2] + in_xz + in_yz - third - square[2]
    s_xy = pair[3] - pair[4] - flux[0] * speed[1]
    s_xz = pair[5] - pair[6] - flux[0] * speed[2]
    s_yz = pair[7] - pair[8] - flux[1] * speed[2]
    magnitude = (s_xx * s_xx + s_yy * s_yy + s_zz * s_zz) + 2.0 * (
        s_xy * s_xy + s_xz * s_xz + s_yz * s_yz
    )
    root = jnp.sqrt(
        relax_base * relax_base
        + (18.0 * math.sqrt(2.0) * smagorinsky_sq) * jnp.sqrt(magnitude) * inverse
    )
    rate = jnp.where(solid == 1, 0.0, 2.0 / (relax_base + root))
    keep = 1.0 - rate
    base = density - 1.5 * (square[0] + square[1] + square[2])
    by_axis = rate * (1.0 / 18.0)
    by_edge = rate * (1.0 / 36.0)
    triple = [3.0 * j for j in flux]
    out = [keep * f[0] + (rate * (1.0 / 3.0)) * base]
    for i in range(1, 19, 2):
        c = lattice_c[i]
        along = moved = None
        for axis in range(3):
            if c[axis] == 0:
                continue
            if along is None:
                along, moved = speed[axis], triple[axis]
            elif c[axis] > 0:
                along, moved = along + speed[axis], moved + triple[axis]
            else:
                along, moved = along - speed[axis], moved - triple[axis]
        even = base + 1.5 * (moved * along)
        weight = by_axis if i < 7 else by_edge
        out.append(keep * f[i] + weight * (even + moved))
        out.append(keep * f[i + 1] + weight * (even - moved))
    return out


def kernel(
    n,
    frame_ref,
    f_hbm,
    solid_hbm,
    flags_hbm,
    cells_ref,
    pod_ref,
    mri_ref,
    out_hbm,
    inflow_ref,
    f_buf,
    solid_buf,
    flags_buf,
    r_buf,
    low,
    high,
    part_send,
    part_recv,
    line_send,
    line_recv,
    in_sem,
    mask_sem,
    out_sem,
    part_ssem,
    part_rsem,
    line_ssem,
    line_rsem,
    up_ssem,
    up_rsem,
    down_ssem,
    down_rsem,
):
    planes, height, width = solid_buf.shape
    steps = STEPS
    frames = mri_ref.shape[1]
    local = mri_ref.shape[2]
    modes = pod_ref.shape[2]
    rep = LANES // local
    groups = n // rep
    chunk = 16
    rows = slice(PAD, PAD + height)
    me = lax.axis_index("ax")

    barrier = pltpu.get_barrier_semaphore()

    def greet(k, carry):
        pl.semaphore_signal(
            barrier, inc=1, device_id={"ax": lax.rem(me + k, n)}, device_id_type=MESH
        )
        return carry

    lax.fori_loop(1, n, greet, 0)

    loads = []
    for z in range(planes):
        loads.append(pltpu.make_async_copy(f_hbm.at[:, z], f_buf.at[:, z], in_sem.at[z]))
    solid_load = pltpu.make_async_copy(solid_hbm, solid_buf, mask_sem.at[0])
    flags_load = pltpu.make_async_copy(flags_hbm, flags_buf, mask_sem.at[1])
    loads[planes - 1].start()
    solid_load.start()
    for z in range(planes - 2, -1, -1):
        loads[z].start()
    flags_load.start()

    row_at = lax.broadcasted_iota(jnp.int32, (8, local), 0)
    frame_at = lax.broadcasted_iota(jnp.int32, (frames, local), 0)
    partial = jnp.zeros((8, modes), jnp.float32)
    for j in range(3):
        chosen = jnp.zeros((8, local), jnp.float32)
        for s in range(steps):
            frame = lax.rem(frame_ref[0] + s, frames)
            line = jnp.sum(jnp.where(frame_at == frame, mri_ref[j], 0.0), axis=0, keepdims=True)
            chosen = jnp.where(row_at == s, line, chosen)
        partial = partial + jnp.dot(
            chosen, pod_ref[j], precision=HIGHEST, preferred_element_type=jnp.float32
        )
    part_send[...] = partial[:steps]
    part_recv[me] = partial[:steps]

    def collide(s, z):
        def at(c, carry):
            r0 = pl.multiple_of(c * chunk, chunk)
            here = pl.ds(r0, chunk)
            there = pl.ds(pl.multiple_of(r0 + PAD, 8), chunk)
            f = [f_buf[i, z, here, :] for i in range(19)]
            relaxed = relax(f, solid_buf[z, here, :])
            for i in range(19):
                r_buf[s, slot_of[i], z, there, :] = relaxed[i]
            return carry

        lax.fori_loop(0, height // chunk, at, 0)

    def up_copy(s):
        return pltpu.make_async_remote_copy(
            src_ref=r_buf.at[s, pl.ds(0, CROSS), planes - 1, pl.ds(PAD, height)],
            dst_ref=low.at[s, :, pl.ds(PAD, height)],
            send_sem=up_ssem.at[s],
            recv_sem=up_rsem.at[s],
            device_id={"ax": lax.rem(me + 1, n)},
            device_id_type=MESH,
        )

    def down_copy(s):
        return pltpu.make_async_remote_copy(
            src_ref=r_buf.at[s, pl.ds(CROSS, CROSS), 0, pl.ds(PAD, height)],
            dst_ref=high.at[s, :, pl.ds(PAD, height)],
            send_sem=down_ssem.at[s],
            recv_sem=down_rsem.at[s],
            device_id={"ax": lax.rem(me + n - 1, n)},
            device_id_type=MESH,
        )

    def part_copy(k):
        return pltpu.make_async_remote_copy(
            src_ref=part_send,
            dst_ref=part_recv.at[me],
            send_sem=part_ssem.at[k],
            recv_sem=part_rsem.at[me],
            device_id={"ax": lax.rem(me + k, n)},
            device_id_type=MESH,
        )

    def part_arrival(source):
        return pltpu.make_async_remote_copy(
            src_ref=part_send,
            dst_ref=part_recv.at[source],
            send_sem=part_ssem.at[0],
            recv_sem=part_rsem.at[source],
            device_id={"ax": lax.rem(me + 1, n)},
            device_id_type=MESH,
        )

    def line_copy(source):
        return pltpu.make_async_remote_copy(
            src_ref=line_send,
            dst_ref=line_recv.at[source],
            send_sem=line_ssem.at[0],
            recv_sem=line_rsem.at[source],
            device_id={"ax": 0},
            device_id_type=MESH,
        )

    def send_up(s):
        @pl.when(me < n - 1)
        def _():
            up_copy(s).start()

    def send_down(s):
        @pl.when(me > 0)
        def _():
            down_copy(s).start()

    def stream(s, z, dirs):
        solid = solid_buf[z] == 1
        for i in dirs:
            step_x, step_y, step_z = lattice_c[i]
            own = r_buf[s, slot_of[i], z, rows, :]
            if i == 0:
                f_buf[i, z] = own
                continue
            moved = slice(PAD - step_y, PAD - step_y + height)
            if 0 <= z - step_z < planes:
                source = r_buf[s, slot_of[i], z - step_z, moved, :]
            elif step_z > 0:
                source = low[s, slot_of[i], moved, :]
            else:
                source = high[s, slot_of[i] - CROSS, moved, :]
            if step_x != 0:
                source = pltpu.roll(source, step_x % width, 1)
            bit = 1 << ((i - 1) % 9)
            linked = (flags_buf[(i - 1) // 9, z] & bit) != 0
            back = r_buf[s, slot_of[opposite_of[i]], z, rows, :]
            f_buf[i, z] = jnp.where(solid, own, jnp.where(linked, back, source))

    def inlet():
        def arrived(k, carry):
            line_copy(k).wait_recv()
            return carry

        lax.fori_loop(1, n, arrived, 0)
        lines = [
            functools.reduce(jnp.add, [line_recv[g * rep + k] for k in range(rep)])
            for g in range(groups)
        ]
        cells = cells_ref[...]
        count = cells.shape[1]
        if width & (width - 1) == 0:
            cell_y = lax.shift_right_logical(cells, width.bit_length() - 1)
            cell_x = cells & (width - 1)
        else:
            cell_y = cells // width
            cell_x = cells - cell_y * width
        at_y = lax.broadcasted_iota(jnp.int32, (height, count), 0) == cell_y
        at_x = lax.broadcasted_iota(jnp.int32, (width, count), 0) == cell_x
        spread = jnp.concatenate(
            [
                jnp.where(
                    at_y, jnp.concatenate([v[j, s : s + 1, :] for v in lines], axis=1), 0.0
                )
                for s in range(steps)
                for j in range(3)
            ],
            axis=0,
        )
        plane = lax.dot_general(
            spread,
            jnp.where(at_x, 1.0, 0.0),
            (((1,), (1,)), ((), ())),
            precision=HIGHEST,
            preferred_element_type=jnp.float32,
        )
        for s in range(steps):
            v = [
                inflow_scale * plane[(3 * s + j) * height : (3 * s + j + 1) * height]
                for j in range(3)
            ]
            speed_sq = v[0] * v[0] + v[1] * v[1] + v[2] * v[2]
            for k, i in enumerate(up_dirs):
                along = v[2]
                for axis in range(2):
                    if lattice_c[i][axis] > 0:
                        along = along + v[axis]
                    elif lattice_c[i][axis] < 0:
                        along = along - v[axis]
                low[s, k, rows, :] = lattice_w[i] * (
                    1.0 + 3.0 * along + 4.5 * along * along - 1.5 * speed_sq
                )

    loads[planes - 1].wait()
    solid_load.wait()
    collide(0, planes - 1)
    pl.semaphore_wait(barrier, n - 1)

    def part_start(k, carry):
        part_copy(k).start()
        return carry

    lax.fori_loop(1, n, part_start, 0)
    send_up(0)
    for z in range(planes - 2, -1, -1):
        loads[z].wait()
        collide(0, z)
    send_down(0)
    flags_load.wait()

    for s in range(steps):
        last = s == steps - 1
        for z in range(planes - 1, -1, -1):
            early = [
                i
                for i in range(19)
                if lattice_c[i][2] == 0 or 0 <= z - lattice_c[i][2] < planes
            ]
            stream(s, z, early)
        if s == 0:
            def part_wait(k, carry):
                part_arrival(lax.rem(me + k, n)).wait_recv()
                return carry

            lax.fori_loop(1, n, part_wait, 0)
            total = jnp.sum(part_recv[...], axis=0)
            total = jnp.concatenate([total, jnp.zeros((8 - steps, modes), jnp.float32)], axis=0)
            basis = jnp.concatenate([pod_ref[j] for j in range(3) for _ in range(rep)], axis=0)
            lines = lax.dot_general(
                total,
                basis,
                (((1,), (1,)), ((), ())),
                precision=HIGHEST,
                preferred_element_type=jnp.float32,
            )
            lane = lax.broadcasted_iota(jnp.int32, (steps, LANES), 1)
            first = lax.rem(me, rep) * local
            mine = (lane >= first) & (lane < first + local)
            for j in range(3):
                line = lines[:steps, j * LANES : (j + 1) * LANES]
                inflow_ref[j] = line[:, :local]
                line_send[j] = jnp.where(mine, line, 0.0)

            @pl.when(me == 0)
            def _():
                line_recv[0] = line_send[...]

            @pl.when(me > 0)
            def _():
                line_copy(me).start()

        for z in range(planes - 1, -1, -1):
            if z == planes - 1:

                @pl.when(me < n - 1)
                def _():
                    down_copy(s).wait_recv()

                @pl.when(me == n - 1)
                def _():
                    for k in range(CROSS):
                        high[s, k, rows, :] = r_buf[s, CROSS + k, planes - 1, rows, :]

                stream(s, z, down_dirs)
            if z == 0:
                if s == 0:
                    pl.when(me == 0)(inlet)

                @pl.when(me > 0)
                def _():
                    up_copy(s).wait_recv()

                stream(s, z, up_dirs)
            if last:
                pltpu.make_async_copy(f_buf.at[:, z], out_hbm.at[:, z], out_sem.at[z]).start()
            else:
                collide(s + 1, z)
                if z == planes - 1:
                    send_up(s + 1)
                if z == 0:
                    send_down(s + 1)

    def part_done(k, carry):
        part_copy(k).wait_send()
        return carry

    lax.fori_loop(1, n, part_done, 0)

    @pl.when(me > 0)
    def _():
        line_copy(me).wait_send()
        for s in range(steps):
            down_copy(s).wait_send()

    @pl.when(me < n - 1)
    def _():
        for s in range(steps):
            up_copy(s).wait_send()

    for z in range(planes):
        pltpu.make_async_copy(f_buf.at[:, z], out_hbm.at[:, z], out_sem.at[z]).wait()


def body(n, populations, solid_mask, link_flags, inlet_cells, pod_basis, mri_frames, frame_index):
    planes, height, width = solid_mask.shape
    modes, _, local = pod_basis.shape
    if planes < 2 or LANES % local or n % (LANES // local) or width != LANES or height % 16:
        raise ValueError("sizes")
    dma = pltpu.SemaphoreType.DMA
    f32 = jnp.float32
    advanced, inflow = pl.pallas_call(
        functools.partial(kernel, n),
        name="lattice",
        out_shape=(
            jax.ShapeDtypeStruct(populations.shape, f32),
            jax.ShapeDtypeStruct((3, STEPS, local), f32),
        ),
        in_specs=[
            pl.BlockSpec(memory_space=pltpu.SMEM),
            pl.BlockSpec(memory_space=pl.ANY),
            pl.BlockSpec(memory_space=pl.ANY),
            pl.BlockSpec(memory_space=pl.ANY),
            pl.BlockSpec(memory_space=pltpu.VMEM),
            pl.BlockSpec(memory_space=pltpu.VMEM),
            pl.BlockSpec(memory_space=pltpu.VMEM),
        ],
        out_specs=(
            pl.BlockSpec(memory_space=pl.ANY),
            pl.BlockSpec(memory_space=pltpu.VMEM),
        ),
        scratch_shapes=[
            pltpu.VMEM((19, planes, height, width), f32),
            pltpu.VMEM((planes, height, width), jnp.int32),
            pltpu.VMEM((2, planes, height, width), jnp.int32),
            pltpu.VMEM((STEPS, 19, planes, height + 2 * PAD, width), f32),
            pltpu.VMEM((STEPS, CROSS, height + 2 * PAD, width), f32),
            pltpu.VMEM((STEPS, CROSS, height + 2 * PAD, width), f32),
            pltpu.VMEM((STEPS, modes), f32),
            pltpu.VMEM((n, STEPS, modes), f32),
            pltpu.VMEM((3, STEPS, LANES), f32),
            pltpu.VMEM((n, 3, STEPS, LANES), f32),
            dma((planes,)),
            dma((2,)),
            dma((planes,)),
            dma((n,)),
            dma((n,)),
            dma((1,)),
            dma((n,)),
            dma((STEPS,)),
            dma((STEPS,)),
            dma((STEPS,)),
            dma((STEPS,)),
        ],
        compiler_params=pltpu.CompilerParams(collective_id=0, has_side_effects=True),
    )(
        frame_index,
        populations,
        solid_mask,
        link_flags,
        inlet_cells.reshape(1, -1),
        jnp.transpose(pod_basis, (1, 2, 0)),
        jnp.transpose(mri_frames, (1, 0, 2)),
    )
    return advanced, jnp.transpose(inflow, (1, 0, 2))


def solution(mesh):
    in_specs = (
        P(None, "ax", "case", None),
        P("ax", "case", None),
        P(None, "ax", "case", None),
        P("case"),
        P(None, None, "ax"),
        P(None, "case", "ax"),
        P(),
    )
    out_specs = (P(None, "ax", "case", None), P(None, "case", "ax"))
    return jax.shard_map(
        functools.partial(body, mesh.shape["ax"]),
        mesh=mesh,
        in_specs=in_specs,
        out_specs=out_specs,
        check_vma=False,
    )
```

time: 147 us -> 24.4 us (0.17)
  the two profiles are of different devices: /device:TPU:1 before, /device:TPU:0 now
where the time goes in v1:
time: 24.4 us; the launch traced here: 24.2 us
  Pallas kernels  19.9 us (82%)
  local copies, waits for them, and re-layouts  3.05 us (12%)
  between operations  1.3 us (5%)
    pallas_call x1, Pallas kernels, body(): pl.pallas_call(functools.partial(kernel, n), name='lattice', out_shape=(j...  19.9 us
    unnamed x4, local copies, waits for them, and re-layouts  3.05 us

profile of v1, /device:TPU:0, one launch (start us, length us, event | category | flops | bytes accessed | tf_op | source)
XLA Modules:
  0.0 24.2 jit_solution(1842078151365395722)
XLA Ops:
  1.3 19.9 %lattice.1 = (f32[19,2,64,128]{3,2,1,0:T(8,128)}, f32[3,2,32]{2,1,0:T(2,128)}) custom-call(s32[1]{0:T(128)S(6)} %copy.11.frame_ref, f32[19,2,64,128]{3,2,1,0:T(8,128)} %f_hbm.1, s32[2,64,128]{2,1,0:T(8,128)} %solid_hbm.1, s32[2,2,64,128]{3,2,1,0:T(8,128)} %flags_hbm.1, s32[1,512]{1,0:T(1,128)} %bitcast.7, f32[3,32,512]{2,1,0:T(8,128)} %bitcast.4, ...), custom_call_target="tpu_custom_call" | custom-call | tf_op jit(solution)/shard_map/lattice/pallas_call | solution.py:452
  21.2 0.0 copy-start
  21.2 2.5 %copy.12 = f32[19,2,64,128]{3,2,1,0:T(8,128)} copy(f32[19,2,64,128]{3,2,1,0:T(8,128)} %get-tuple-element.8) | data formatting | bytes 2490368
  23.7 0.0 copy-done
  23.7 0.6 %copy.13 = f32[2,3,32]{2,0,1:T(2,128)} copy(f32[2,3,32]{2,0,1:T(2,128)S(1)} %bitcast.6) | data formatting | bytes 1536
Async XLA Ops:
  21.2 2.5 %copy-start = (f32[3,2,32]{2,1,0:T(2,128)S(1)}, f32[3,2,32]{2,1,0:T(2,128)}, u32[]{:S(2)}) copy-start(f32[3,2,32]{2,1,0:T(2,128)} %get-tuple-element.5) | copy-start | bytes 2308

commit v2 on v1

--- a/solution.py
+++ b/solution.py
@@ -10,7 +10,6 @@
 
 STEPS = 2
 MESH = pl.DeviceIdType.MESH
-HIGHEST = lax.Precision.HIGHEST
 PAD = 8
 LANES = 128
 
@@ -48,6 +47,19 @@
 CROSS = len(up_dirs)
 
 
+def split_dot(left, right, dims):
+    dot = functools.partial(
+        lax.dot_general, dimension_numbers=dims, preferred_element_type=jnp.float32
+    )
+    rows = left.shape[0]
+    left_high = left.astype(jnp.bfloat16)
+    left_low = (left - left_high.astype(jnp.float32)).astype(jnp.bfloat16)
+    right_high = right.astype(jnp.bfloat16)
+    right_low = (right - right_high.astype(jnp.float32)).astype(jnp.bfloat16)
+    both = dot(jnp.concatenate([left_high, left_low], axis=0), right_high)
+    return both[:rows] + (both[rows:] + dot(left_high, right_low))
+
+
 def relax(f, solid):
     pair = [f[i] + f[i + 1] for i in range(1, 19, 2)]
     diff = [f[i] - f[i + 1] for i in range(1, 19, 2)]
@@ -105,16 +117,21 @@
 
 def kernel(
     n,
-    frame_ref,
+    frame_hbm,
     f_hbm,
     solid_hbm,
     flags_hbm,
+    cells_hbm,
+    pod_hbm,
+    mri_hbm,
+    f_buf,
+    inflow_ref,
+    frame_ref,
     cells_ref,
     pod_ref,
     mri_ref,
-    out_hbm,
-    inflow_ref,
-    f_buf,
+    at_y,
+    at_x,
     solid_buf,
     flags_buf,
     r_buf,
@@ -126,7 +143,6 @@
     line_recv,
     in_sem,
     mask_sem,
-    out_sem,
     part_ssem,
     part_rsem,
     line_ssem,
@@ -162,11 +178,22 @@
         loads.append(pltpu.make_async_copy(f_hbm.at[:, z], f_buf.at[:, z], in_sem.at[z]))
     solid_load = pltpu.make_async_copy(solid_hbm, solid_buf, mask_sem.at[0])
     flags_load = pltpu.make_async_copy(flags_hbm, flags_buf, mask_sem.at[1])
+    pod_load = pltpu.make_async_copy(pod_hbm, pod_ref, mask_sem.at[2])
+    mri_load = pltpu.make_async_copy(mri_hbm, mri_ref, mask_sem.at[3])
+    cells_load = pltpu.make_async_copy(cells_hbm, cells_ref, mask_sem.at[4])
+    frame_load = pltpu.make_async_copy(frame_hbm, frame_ref, mask_sem.at[5])
+    frame_load.start()
+    mri_load.start()
+    pod_load.start()
     loads[planes - 1].start()
     solid_load.start()
     for z in range(planes - 2, -1, -1):
         loads[z].start()
     flags_load.start()
+    cells_load.start()
+    frame_load.wait()
+    mri_load.wait()
+    pod_load.wait()
 
     row_at = lax.broadcasted_iota(jnp.int32, (8, local), 0)
     frame_at = lax.broadcasted_iota(jnp.int32, (frames, local), 0)
@@ -177,11 +204,8 @@
             frame = lax.rem(frame_ref[0] + s, frames)
             line = jnp.sum(jnp.where(frame_at == frame, mri_ref[j], 0.0), axis=0, keepdims=True)
             chosen = jnp.where(row_at == s, line, chosen)
-        partial = partial + jnp.dot(
-            chosen, pod_ref[j], precision=HIGHEST, preferred_element_type=jnp.float32
-        )
+        partial = partial + split_dot(chosen, pod_ref[j], (((1,), (0,)), ((), ())))
     part_send[...] = partial[:steps]
-    part_recv[me] = partial[:steps]
 
     def collide(s, z):
         def at(c, carry):
@@ -219,19 +243,19 @@
     def part_copy(k):
         return pltpu.make_async_remote_copy(
             src_ref=part_send,
-            dst_ref=part_recv.at[me],
-            send_sem=part_ssem.at[k],
-            recv_sem=part_rsem.at[me],
+            dst_ref=part_recv.at[k - 1],
+            send_sem=part_ssem.at[0],
+            recv_sem=part_rsem.at[0],
             device_id={"ax": lax.rem(me + k, n)},
             device_id_type=MESH,
         )
 
-    def part_arrival(source):
+    def all_parts():
         return pltpu.make_async_remote_copy(
-            src_ref=part_send,
-            dst_ref=part_recv.at[source],
+            src_ref=part_recv,
+            dst_ref=part_recv,
             send_sem=part_ssem.at[0],
-            recv_sem=part_rsem.at[source],
+            recv_sem=part_rsem.at[0],
             device_id={"ax": lax.rem(me + 1, n)},
             device_id_type=MESH,
         )
@@ -239,9 +263,9 @@
     def line_copy(source):
         return pltpu.make_async_remote_copy(
             src_ref=line_send,
-            dst_ref=line_recv.at[source],
+            dst_ref=line_recv.at[source - 1],
             send_sem=line_ssem.at[0],
-            recv_sem=line_rsem.at[source],
+            recv_sem=line_rsem.at[0],
             device_id={"ax": 0},
             device_id_type=MESH,
         )
@@ -278,16 +302,17 @@
             back = r_buf[s, slot_of[opposite_of[i]], z, rows, :]
             f_buf[i, z] = jnp.where(solid, own, jnp.where(linked, back, source))
 
-    def inlet():
-        def arrived(k, carry):
-            line_copy(k).wait_recv()
-            return carry
-
-        lax.fori_loop(1, n, arrived, 0)
-        lines = [
-            functools.reduce(jnp.add, [line_recv[g * rep + k] for k in range(rep)])
-            for g in range(groups)
-        ]
+    def all_lines():
+        return pltpu.make_async_remote_copy(
+            src_ref=line_recv,
+            dst_ref=line_recv,
+            send_sem=line_ssem.at[0],
+            recv_sem=line_rsem.at[0],
+            device_id={"ax": lax.rem(me + 1, n)},
+            device_id_type=MESH,
+        )
+
+    def one_hot():
         cells = cells_ref[...]
         count = cells.shape[1]
         if width & (width - 1) == 0:
@@ -296,28 +321,48 @@
         else:
             cell_y = cells // width
             cell_x = cells - cell_y * width
-        at_y = lax.broadcasted_iota(jnp.int32, (height, count), 0) == cell_y
-        at_x = lax.broadcasted_iota(jnp.int32, (width, count), 0) == cell_x
-        spread = jnp.concatenate(
+        rows_y = lax.broadcasted_iota(jnp.int32, (height, count), 0) == cell_y
+        rows_x = lax.broadcasted_iota(jnp.int32, (width, count), 0) == cell_x
+        at_y[...] = jnp.where(rows_y, 1.0, 0.0).astype(jnp.bfloat16)
+        at_x[...] = jnp.where(rows_x, 1.0, 0.0).astype(jnp.bfloat16)
+
+    def inlet():
+        all_lines().wait_recv()
+        own = line_send[...]
+        received = [own] + [line_recv[k] for k in range(n - 1)]
+        lines = [
+            functools.reduce(jnp.add, received[g * rep : (g + 1) * rep]) for g in range(groups)
+        ]
+        count = at_y.shape[1]
+        lit = at_y[...]
+        terms = []
+        rest = jnp.concatenate(
             [
-                jnp.where(
-                    at_y, jnp.concatenate([v[j, s : s + 1, :] for v in lines], axis=1), 0.0
-                )
-                for s in range(steps)
+                jnp.concatenate([v[j] for v in lines], axis=1)
                 for j in range(3)
-            ],
+            ]
+            + [jnp.zeros((8 - 3 * steps, count), jnp.float32)] * (3 * steps < 8),
             axis=0,
         )
-        plane = lax.dot_general(
-            spread,
-            jnp.where(at_x, 1.0, 0.0),
+        for _ in range(3):
+            head = rest.astype(jnp.bfloat16)
+            rest = rest - head.astype(jnp.float32)
+            head = head.astype(jnp.float32)
+            terms += [
+                lit * jnp.broadcast_to(head[r : r + 1], lit.shape).astype(jnp.bfloat16)
+                for r in range(3 * steps)
+            ]
+        found = lax.dot_general(
+            jnp.concatenate(terms, axis=0),
+            at_x[...],
             (((1,), (1,)), ((), ())),
-            precision=HIGHEST,
             preferred_element_type=jnp.float32,
         )
+        size = 3 * steps * height
+        plane = found[:size] + (found[size : 2 * size] + found[2 * size :])
         for s in range(steps):
             v = [
-                inflow_scale * plane[(3 * s + j) * height : (3 * s + j + 1) * height]
+                inflow_scale * plane[(steps * j + s) * height : (steps * j + s + 1) * height]
                 for j in range(3)
             ]
             speed_sq = v[0] * v[0] + v[1] * v[1] + v[2] * v[2]
@@ -335,6 +380,7 @@
     loads[planes - 1].wait()
     solid_load.wait()
     collide(0, planes - 1)
+    cells_load.wait()
     pl.semaphore_wait(barrier, n - 1)
 
     def part_start(k, carry):
@@ -348,43 +394,39 @@
         collide(0, z)
     send_down(0)
     flags_load.wait()
-
+    pl.when(me == 0)(one_hot)
+
+    def early(s, z, flat):
+        dirs = [
+            i
+            for i in range(19)
+            if (lattice_c[i][2] == 0) == flat and 0 <= z - lattice_c[i][2] < planes
+        ]
+        stream(s, z, dirs)
+
+    for z in range(planes):
+        early(0, z, True)
     for s in range(steps):
         last = s == steps - 1
         for z in range(planes - 1, -1, -1):
-            early = [
-                i
-                for i in range(19)
-                if lattice_c[i][2] == 0 or 0 <= z - lattice_c[i][2] < planes
-            ]
-            stream(s, z, early)
+            early(s, z, False)
         if s == 0:
-            def part_wait(k, carry):
-                part_arrival(lax.rem(me + k, n)).wait_recv()
-                return carry
-
-            lax.fori_loop(1, n, part_wait, 0)
-            total = jnp.sum(part_recv[...], axis=0)
+            all_parts().wait_recv()
+            total = part_send[...] + jnp.sum(part_recv[...], axis=0)
             total = jnp.concatenate([total, jnp.zeros((8 - steps, modes), jnp.float32)], axis=0)
-            basis = jnp.concatenate([pod_ref[j] for j in range(3) for _ in range(rep)], axis=0)
-            lines = lax.dot_general(
-                total,
-                basis,
-                (((1,), (1,)), ((), ())),
-                precision=HIGHEST,
-                preferred_element_type=jnp.float32,
-            )
+            basis = jnp.concatenate([pod_ref[j] for j in range(3)], axis=0)
+            if 3 * local < LANES:
+                basis = jnp.concatenate(
+                    [basis, jnp.zeros((LANES - 3 * local, modes), jnp.float32)], axis=0
+                )
+            lines = split_dot(total, basis, (((1,), (1,)), ((), ())))
             lane = lax.broadcasted_iota(jnp.int32, (steps, LANES), 1)
             first = lax.rem(me, rep) * local
             mine = (lane >= first) & (lane < first + local)
             for j in range(3):
-                line = lines[:steps, j * LANES : (j + 1) * LANES]
-                inflow_ref[j] = line[:, :local]
-                line_send[j] = jnp.where(mine, line, 0.0)
-
-            @pl.when(me == 0)
-            def _():
-                line_recv[0] = line_send[...]
+                inflow_ref[j] = lines[:steps, j * local : (j + 1) * local]
+                turn = lax.rem(first + (LANES - j * local), LANES)
+                line_send[j] = jnp.where(mine, pltpu.roll(lines, turn, 1)[:steps], 0.0)
 
             @pl.when(me > 0)
             def _():
@@ -412,20 +454,15 @@
                     up_copy(s).wait_recv()
 
                 stream(s, z, up_dirs)
-            if last:
-                pltpu.make_async_copy(f_buf.at[:, z], out_hbm.at[:, z], out_sem.at[z]).start()
-            else:
+            if not last:
                 collide(s + 1, z)
                 if z == planes - 1:
                     send_up(s + 1)
                 if z == 0:
                     send_down(s + 1)
-
-    def part_done(k, carry):
-        part_copy(k).wait_send()
-        return carry
-
-    lax.fori_loop(1, n, part_done, 0)
+                early(s + 1, z, True)
+
+    all_parts().wait_send()
 
     @pl.when(me > 0)
     def _():
@@ -438,8 +475,16 @@
         for s in range(steps):
             up_copy(s).wait_send()
 
-    for z in range(planes):
-        pltpu.make_async_copy(f_buf.at[:, z], out_hbm.at[:, z], out_sem.at[z]).wait()
+
+def finish(f_ref, inflow_ref, out_hbm, inflow_hbm, sem):
+    copies = [
+        pltpu.make_async_copy(f_ref, out_hbm, sem.at[0]),
+        pltpu.make_async_copy(inflow_ref, inflow_hbm, sem.at[1]),
+    ]
+    for copy in copies:
+        copy.start()
+    for copy in copies:
+        copy.wait()
 
 
 def body(n, populations, solid_mask, link_flags, inlet_cells, pod_basis, mri_frames, frame_index):
@@ -449,50 +494,48 @@
         raise ValueError("sizes")
     dma = pltpu.SemaphoreType.DMA
     f32 = jnp.float32
+    wide = pltpu.CompilerParams(vmem_limit_bytes=32 * 1024 * 1024)
+    on_chip = pl.BlockSpec(memory_space=pltpu.VMEM)
+    anywhere = pl.BlockSpec(memory_space=pl.ANY)
     advanced, inflow = pl.pallas_call(
         functools.partial(kernel, n),
         name="lattice",
         out_shape=(
-            jax.ShapeDtypeStruct(populations.shape, f32),
-            jax.ShapeDtypeStruct((3, STEPS, local), f32),
+            pltpu.VMEM(populations.shape, f32),
+            pltpu.VMEM((3, STEPS, local), f32),
         ),
-        in_specs=[
-            pl.BlockSpec(memory_space=pltpu.SMEM),
-            pl.BlockSpec(memory_space=pl.ANY),
-            pl.BlockSpec(memory_space=pl.ANY),
-            pl.BlockSpec(memory_space=pl.ANY),
-            pl.BlockSpec(memory_space=pltpu.VMEM),
-            pl.BlockSpec(memory_space=pltpu.VMEM),
-            pl.BlockSpec(memory_space=pltpu.VMEM),
-        ],
-        out_specs=(
-            pl.BlockSpec(memory_space=pl.ANY),
-            pl.BlockSpec(memory_space=pltpu.VMEM),
-        ),
+        in_specs=[pl.BlockSpec(memory_space=pltpu.HBM)] * 7,
+        out_specs=(on_chip, on_chip),
         scratch_shapes=[
-            pltpu.VMEM((19, planes, height, width), f32),
+            pltpu.SMEM((1,), jnp.int32),
+            pltpu.VMEM((1, inlet_cells.shape[0]), jnp.int32),
+            pltpu.VMEM((3, local, modes), f32),
+            pltpu.VMEM((3, mri_frames.shape[0], local), f32),
+            pltpu.VMEM((height, inlet_cells.shape[0]), jnp.bfloat16),
+            pltpu.VMEM((width, inlet_cells.shape[0]), jnp.bfloat16),
             pltpu.VMEM((planes, height, width), jnp.int32),
             pltpu.VMEM((2, planes, height, width), jnp.int32),
             pltpu.VMEM((STEPS, 19, planes, height + 2 * PAD, width), f32),
             pltpu.VMEM((STEPS, CROSS, height + 2 * PAD, width), f32),
             pltpu.VMEM((STEPS, CROSS, height + 2 * PAD, width), f32),
             pltpu.VMEM((STEPS, modes), f32),
-            pltpu.VMEM((n, STEPS, modes), f32),
+            pltpu.VMEM((n - 1, STEPS, modes), f32),
             pltpu.VMEM((3, STEPS, LANES), f32),
-            pltpu.VMEM((n, 3, STEPS, LANES), f32),
+            pltpu.VMEM((n - 1, 3, STEPS, LANES), f32),
             dma((planes,)),
-            dma((2,)),
-            dma((planes,)),
-            dma((n,)),
-            dma((n,)),
+            dma((6,)),
             dma((1,)),
-            dma((n,)),
+            dma((1,)),
+            dma((1,)),
+            dma((1,)),
             dma((STEPS,)),
             dma((STEPS,)),
             dma((STEPS,)),
             dma((STEPS,)),
         ],
-        compiler_params=pltpu.CompilerParams(collective_id=0, has_side_effects=True),
+        compiler_params=pltpu.CompilerParams(
+            collective_id=0, has_side_effects=True, vmem_limit_bytes=32 * 1024 * 1024
+        ),
     )(
         frame_index,
         populations,
@@ -502,6 +545,18 @@
         jnp.transpose(pod_basis, (1, 2, 0)),
         jnp.transpose(mri_frames, (1, 0, 2)),
     )
+    advanced, inflow = pl.pallas_call(
+        finish,
+        name="finish",
+        out_shape=(
+            jax.ShapeDtypeStruct(populations.shape, f32),
+            jax.ShapeDtypeStruct((3, STEPS, local), f32),
+        ),
+        in_specs=[on_chip, on_chip],
+        out_specs=(anywhere, anywhere),
+        scratch_shapes=[dma((2,))],
+        compiler_params=wide,
+    )(advanced, inflow)
     return advanced, jnp.transpose(inflow, (1, 0, 2))
 
 

time: 24.4 us -> 24.7 us (1.012)
  the two profiles are of different devices: /device:TPU:0 before, /device:TPU:1 now
where the time goes in v2:
time: 24.7 us; the launch traced here: 24.4 us
  Pallas kernels  17.7 us (72%)
  local copies, waits for them, and re-layouts  5.4 us (22%)
  between operations  1.3 us (5%)
    pallas_call x1, Pallas kernels, body(): pl.pallas_call(functools.partial(kernel, n), name='lattice', out_shape=(p...  16.6 us
    unnamed x12, local copies, waits for them, and re-layouts  5.4 us
    pallas_call x1, Pallas kernels, body(): pl.pallas_call(finish, name='finish', out_shape=(jax.ShapeDtypeStruct(pop...  1.06 us

profile of v2, /device:TPU:1, one launch (start us, length us, event | category | flops | bytes accessed | tf_op | source)
XLA Modules:
  0.0 24.4 jit_solution(16091414630948705957)
XLA Ops:
  1.3 0.0 copy-start
  1.3 1.3 %copy-done = f32[19,2,64,128]{3,2,1,0:T(8,128)S(1)} copy-done((f32[19,2,64,128]{3,2,1,0:T(8,128)S(1)}, f32[19,2,64,128]{3,2,1,0:T(8,128)}, u32[]{:S(2)}) %copy-start) | copy-done | bytes 1245208
  2.6 0.0 copy-start.1
  2.6 0.9 %copy-done.1 = f32[512,3,32]{0,2,1:T(8,128)S(1)} copy-done((f32[512,3,32]{0,2,1:T(8,128)S(1)}, f32[512,3,32]{0,2,1:T(8,128)}, u32[]{:S(2)}) %copy-start.1) | copy-done | bytes 196632
  3.5 0.0 copy-start.2
  3.5 0.9 %copy-done.2 = s32[2,2,64,128]{3,2,1,0:T(8,128)S(1)} copy-done((s32[2,2,64,128]{3,2,1,0:T(8,128)S(1)}, s32[2,2,64,128]{3,2,1,0:T(8,128)}, u32[]{:S(2)}) %copy-start.2) | copy-done | bytes 131096
  4.4 0.0 copy-start.3
  4.4 0.8 %copy-done.3 = s32[2,64,128]{2,1,0:T(8,128)S(1)} copy-done((s32[2,64,128]{2,1,0:T(8,128)S(1)}, s32[2,64,128]{2,1,0:T(8,128)}, u32[]{:S(2)}) %copy-start.3) | copy-done | bytes 65560
  5.2 0.0 copy-start.4
  5.2 0.8 %copy-done.4 = f32[24,3,32]{2,0,1:T(8,128)S(1)} copy-done((f32[24,3,32]{2,0,1:T(8,128)S(1)}, f32[24,3,32]{2,0,1:T(8,128)}, u32[]{:S(2)}) %copy-start.4) | copy-done | bytes 9240
  6.0 0.0 copy-start.5
  6.0 0.7 %copy-done.5 = s32[512]{0:T(512)S(1)} copy-done((s32[512]{0:T(512)S(1)}, s32[512]{0:T(512)}, u32[]{:S(2)}) %copy-start.5) | copy-done | bytes 2072
  6.7 16.6 %lattice.1 = (f32[19,2,64,128]{3,2,1,0:T(8,128)S(1)}, f32[3,2,32]{2,1,0:T(2,128)S(1)}) custom-call(s32[1]{0:T(128)S(6)} %copy.9.frame_hbm, f32[19,2,64,128]{3,2,1,0:T(8,128)S(1)} %copy-done, s32[2,64,128]{2,1,0:T(8,128)S(1)} %copy-done.3, s32[2,2,64,128]{3,2,1,0:T(8,128)S(1)} %copy-done.2, s32[1,512]{1,0:T(1,128)S(1)} %bitcast.6, f32[3,32,512]{2,1,0:T(8,128)S(1)} %bitcast.4, ...), custom_call_target="tpu_custom_call" | custom-call | tf_op jit(solution)/shard_map/lattice/pallas_call | solution.py:500
  23.3 1.1 %finish.1 = (f32[19,2,64,128]{3,2,1,0:T(8,128)}, f32[3,2,32]{2,1,0:T(2,128)}) custom-call(f32[19,2,64,128]{3,2,1,0:T(8,128)S(1)} %get-tuple-element.6.f_ref, f32[3,2,32]{2,1,0:T(2,128)S(1)} %get-tuple-element.7.inflow_ref), custom_call_target="tpu_custom_call" | custom-call | tf_op jit(solution)/shard_map/finish/pallas_call | solution.py:548
Async XLA Ops:
  1.3 1.3 %copy-start = (f32[19,2,64,128]{3,2,1,0:T(8,128)S(1)}, f32[19,2,64,128]{3,2,1,0:T(8,128)}, u32[]{:S(2)}) copy-start(f32[19,2,64,128]{3,2,1,0:T(8,128)} %f_hbm.1) | copy-start | bytes 3735556
  2.6 0.9 %copy-start.1 = (f32[512,3,32]{0,2,1:T(8,128)S(1)}, f32[512,3,32]{0,2,1:T(8,128)}, u32[]{:S(2)}) copy-start(f32[512,3,32]{0,2,1:T(8,128)} %param.11) | copy-start | bytes 589828
  3.5 0.9 %copy-start.2 = (s32[2,2,64,128]{3,2,1,0:T(8,128)S(1)}, s32[2,2,64,128]{3,2,1,0:T(8,128)}, u32[]{:S(2)}) copy-start(s32[2,2,64,128]{3,2,1,0:T(8,128)} %flags_hbm.1) | copy-start | bytes 393220
  4.4 0.8 %copy-start.3 = (s32[2,64,128]{2,1,0:T(8,128)S(1)}, s32[2,64,128]{2,1,0:T(8,128)}, u32[]{:S(2)}) copy-start(s32[2,64,128]{2,1,0:T(8,128)} %solid_hbm.1) | copy-start | bytes 196612
  5.2 0.8 %copy-start.4 = (f32[24,3,32]{2,0,1:T(8,128)S(1)}, f32[24,3,32]{2,0,1:T(8,128)}, u32[]{:S(2)}) copy-start(f32[24,3,32]{2,0,1:T(8,128)} %param.12) | copy-start | bytes 27652
  6.0 0.7 %copy-start.5 = (s32[512]{0:T(512)S(1)}, s32[512]{0:T(512)}, u32[]{:S(2)}) copy-start(s32[512]{0:T(512)} %param.10) | copy-start | bytes 6148

commit v3 on v2

--- a/solution.py
+++ b/solution.py
@@ -117,7 +117,7 @@
 
 def kernel(
     n,
-    frame_hbm,
+    frame_ref,
     f_hbm,
     solid_hbm,
     flags_hbm,
@@ -126,7 +126,6 @@
     mri_hbm,
     f_buf,
     inflow_ref,
-    frame_ref,
     cells_ref,
     pod_ref,
     mri_ref,
@@ -181,8 +180,6 @@
     pod_load = pltpu.make_async_copy(pod_hbm, pod_ref, mask_sem.at[2])
     mri_load = pltpu.make_async_copy(mri_hbm, mri_ref, mask_sem.at[3])
     cells_load = pltpu.make_async_copy(cells_hbm, cells_ref, mask_sem.at[4])
-    frame_load = pltpu.make_async_copy(frame_hbm, frame_ref, mask_sem.at[5])
-    frame_load.start()
     mri_load.start()
     pod_load.start()
     loads[planes - 1].start()
@@ -191,7 +188,6 @@
         loads[z].start()
     flags_load.start()
     cells_load.start()
-    frame_load.wait()
     mri_load.wait()
     pod_load.wait()
 
@@ -496,6 +492,7 @@
     f32 = jnp.float32
     wide = pltpu.CompilerParams(vmem_limit_bytes=32 * 1024 * 1024)
     on_chip = pl.BlockSpec(memory_space=pltpu.VMEM)
+    in_hbm = pl.BlockSpec(memory_space=pltpu.HBM)
     anywhere = pl.BlockSpec(memory_space=pl.ANY)
     advanced, inflow = pl.pallas_call(
         functools.partial(kernel, n),
@@ -504,10 +501,9 @@
             pltpu.VMEM(populations.shape, f32),
             pltpu.VMEM((3, STEPS, local), f32),
         ),
-        in_specs=[pl.BlockSpec(memory_space=pltpu.HBM)] * 7,
+        in_specs=[pl.BlockSpec(memory_space=pltpu.SMEM)] + [in_hbm] * 6,
         out_specs=(on_chip, on_chip),
         scratch_shapes=[
-            pltpu.SMEM((1,), jnp.int32),
             pltpu.VMEM((1, inlet_cells.shape[0]), jnp.int32),
             pltpu.VMEM((3, local, modes), f32),
             pltpu.VMEM((3, mri_frames.shape[0], local), f32),
@@ -523,7 +519,7 @@
             pltpu.VMEM((3, STEPS, LANES), f32),
             pltpu.VMEM((n - 1, 3, STEPS, LANES), f32),
             dma((planes,)),
-            dma((6,)),
+            dma((5,)),
             dma((1,)),
             dma((1,)),
             dma((1,)),
@@ -538,12 +534,17 @@
         ),
     )(
         frame_index,
-        populations,
-        solid_mask,
-        link_flags,
-        inlet_cells.reshape(1, -1),
-        jnp.transpose(pod_basis, (1, 2, 0)),
-        jnp.transpose(mri_frames, (1, 0, 2)),
+        *(
+            pltpu.with_memory_space_constraint(operand, pltpu.HBM)
+            for operand in (
+                populations,
+                solid_mask,
+                link_flags,
+                inlet_cells.reshape(1, -1),
+                jnp.transpose(pod_basis, (1, 2, 0)),
+                jnp.transpose(mri_frames, (1, 0, 2)),
+            )
+        )
     )
     advanced, inflow = pl.pallas_call(
         finish,

time: 24.7 us -> 19.2 us (0.78)
  local copies, waits for them, and re-layouts: 5.4 us -> 0 us
    unnamed x12 -> x0, local copies, waits for them, and re-layouts: 5.4 us -> none
where the time goes in v3:
time: 19.2 us; the launch traced here: 19 us
  Pallas kernels  17.7 us (92%)
  between operations  1.29 us (7%)
    pallas_call x1, Pallas kernels, body(): pl.pallas_call(functools.partial(kernel, n), name='lattice', out_shape=(p...  16.7 us
    pallas_call x1, Pallas kernels, body(): pl.pallas_call(finish, name='finish', out_shape=(jax.ShapeDtypeStruct(pop...  1.06 us

profile of v3, /device:TPU:1, one launch (start us, length us, event | category | flops | bytes accessed | tf_op | source)
XLA Modules:
  0.0 19.0 jit_solution(5721487667094783067)
XLA Ops:
  1.3 16.7 %lattice.1 = (f32[19,2,64,128]{3,2,1,0:T(8,128)S(1)}, f32[3,2,32]{2,1,0:T(2,128)S(1)}) custom-call(s32[1]{0:T(128)S(6)} %copy.9.frame_ref, f32[19,2,64,128]{3,2,1,0:T(8,128)} %f_hbm.1, s32[2,64,128]{2,1,0:T(8,128)} %solid_hbm.1, s32[2,2,64,128]{3,2,1,0:T(8,128)} %flags_hbm.1, s32[1,512]{1,0:T(1,128)} %bitcast.6, f32[3,32,512]{2,1,0:T(8,128)} %bitcast.4, ...), custom_call_target="tpu_custom_call" | custom-call | tf_op jit(solution)/shard_map/lattice/pallas_call | solution.py:497
  18.0 1.1 %finish.1 = (f32[19,2,64,128]{3,2,1,0:T(8,128)}, f32[3,2,32]{2,1,0:T(2,128)}) custom-call(f32[19,2,64,128]{3,2,1,0:T(8,128)S(1)} %get-tuple-element.6.f_ref, f32[3,2,32]{2,1,0:T(2,128)S(1)} %get-tuple-element.7.inflow_ref), custom_call_target="tpu_custom_call" | custom-call | tf_op jit(solution)/shard_map/finish/pallas_call | solution.py:549

commit v4 on v3

--- a/solution.py
+++ b/solution.py
@@ -375,8 +375,12 @@
 
     loads[planes - 1].wait()
     solid_load.wait()
-    collide(0, planes - 1)
+    for z in range(planes - 1, -1, -1):
+        if z < planes - 1:
+            loads[z].wait()
+        collide(0, z)
     cells_load.wait()
+    pl.when(me == 0)(one_hot)
     pl.semaphore_wait(barrier, n - 1)
 
     def part_start(k, carry):
@@ -385,12 +389,8 @@
 
     lax.fori_loop(1, n, part_start, 0)
     send_up(0)
-    for z in range(planes - 2, -1, -1):
-        loads[z].wait()
-        collide(0, z)
     send_down(0)
     flags_load.wait()
-    pl.when(me == 0)(one_hot)
 
     def early(s, z, flat):
         dirs = [
@@ -473,14 +473,13 @@
 
 
 def finish(f_ref, inflow_ref, out_hbm, inflow_hbm, sem):
-    copies = [
-        pltpu.make_async_copy(f_ref, out_hbm, sem.at[0]),
-        pltpu.make_async_copy(inflow_ref, inflow_hbm, sem.at[1]),
-    ]
-    for copy in copies:
-        copy.start()
-    for copy in copies:
-        copy.wait()
+    count = f_ref.shape[0]
+    small = pltpu.make_async_copy(inflow_ref, inflow_hbm, sem.at[1])
+    small.start()
+    for i in range(count):
+        pltpu.make_async_copy(f_ref.at[i], out_hbm.at[i], sem.at[0]).start()
+    pltpu.make_async_copy(f_ref, out_hbm, sem.at[0]).wait()
+    small.wait()
 
 
 def body(n, populations, solid_mask, link_flags, inlet_cells, pod_basis, mri_frames, frame_index):

time: 19.2 us -> 19.2 us (level)
  no operation moved by 1% of the time
where the time goes in v4:
time: 19.2 us; the launch traced here: 19 us
  Pallas kernels  17.7 us (92%)
  between operations  1.29 us (7%)
    pallas_call x1, Pallas kernels, body(): pl.pallas_call(functools.partial(kernel, n), name='lattice', out_shape=(p...  16.7 us
    pallas_call x1, Pallas kernels, body(): pl.pallas_call(finish, name='finish', out_shape=(jax.ShapeDtypeStruct(pop...  1.03 us

profile of v4, /device:TPU:1, one launch (start us, length us, event | category | flops | bytes accessed | tf_op | source)
XLA Modules:
  0.0 19.0 jit_solution(12424989445925214345)
XLA Ops:
  1.3 16.7 %lattice.1 = (f32[19,2,64,128]{3,2,1,0:T(8,128)S(1)}, f32[3,2,32]{2,1,0:T(2,128)S(1)}) custom-call(s32[1]{0:T(128)S(6)} %copy.9.frame_ref, f32[19,2,64,128]{3,2,1,0:T(8,128)} %f_hbm.1, s32[2,64,128]{2,1,0:T(8,128)} %solid_hbm.1, s32[2,2,64,128]{3,2,1,0:T(8,128)} %flags_hbm.1, s32[1,512]{1,0:T(1,128)} %bitcast.6, f32[3,32,512]{2,1,0:T(8,128)} %bitcast.4, ...), custom_call_target="tpu_custom_call" | custom-call | tf_op jit(solution)/shard_map/lattice/pallas_call | solution.py:496
  18.0 1.0 %finish.1 = (f32[19,2,64,128]{3,2,1,0:T(8,128)}, f32[3,2,32]{2,1,0:T(2,128)}) custom-call(f32[19,2,64,128]{3,2,1,0:T(8,128)S(1)} %get-tuple-element.6.f_ref, f32[3,2,32]{2,1,0:T(2,128)S(1)} %get-tuple-element.7.inflow_ref), custom_call_target="tpu_custom_call" | custom-call | tf_op jit(solution)/shard_map/finish/pallas_call | solution.py:548

commit v5 on v4

--- a/solution.py
+++ b/solution.py
@@ -203,7 +203,7 @@
         partial = partial + split_dot(chosen, pod_ref[j], (((1,), (0,)), ((), ())))
     part_send[...] = partial[:steps]
 
-    def collide(s, z):
+    def collide(s, z, first=0, count=None):
         def at(c, carry):
             r0 = pl.multiple_of(c * chunk, chunk)
             here = pl.ds(r0, chunk)
@@ -214,22 +214,24 @@
                 r_buf[s, slot_of[i], z, there, :] = relaxed[i]
             return carry
 
-        lax.fori_loop(0, height // chunk, at, 0)
-
-    def up_copy(s):
+        lax.fori_loop(first, height // chunk if count is None else first + count, at, 0)
+
+    def up_copy(s, start=0, size=None):
+        span = pl.ds(PAD + start, height if size is None else size)
         return pltpu.make_async_remote_copy(
-            src_ref=r_buf.at[s, pl.ds(0, CROSS), planes - 1, pl.ds(PAD, height)],
-            dst_ref=low.at[s, :, pl.ds(PAD, height)],
+            src_ref=r_buf.at[s, pl.ds(0, CROSS), planes - 1, span],
+            dst_ref=low.at[s, :, span],
             send_sem=up_ssem.at[s],
             recv_sem=up_rsem.at[s],
             device_id={"ax": lax.rem(me + 1, n)},
             device_id_type=MESH,
         )
 
-    def down_copy(s):
+    def down_copy(s, start=0, size=None):
+        span = pl.ds(PAD + start, height if size is None else size)
         return pltpu.make_async_remote_copy(
-            src_ref=r_buf.at[s, pl.ds(CROSS, CROSS), 0, pl.ds(PAD, height)],
-            dst_ref=high.at[s, :, pl.ds(PAD, height)],
+            src_ref=r_buf.at[s, pl.ds(CROSS, CROSS), 0, span],
+            dst_ref=high.at[s, :, span],
             send_sem=down_ssem.at[s],
             recv_sem=down_rsem.at[s],
             device_id={"ax": lax.rem(me + n - 1, n)},
@@ -266,15 +268,15 @@
             device_id_type=MESH,
         )
 
-    def send_up(s):
+    def send_up(s, start=0, size=None):
         @pl.when(me < n - 1)
         def _():
-            up_copy(s).start()
-
-    def send_down(s):
+            up_copy(s, start, size).start()
+
+    def send_down(s, start=0, size=None):
         @pl.when(me > 0)
         def _():
-            down_copy(s).start()
+            down_copy(s, start, size).start()
 
     def stream(s, z, dirs):
         solid = solid_buf[z] == 1
@@ -451,11 +453,12 @@
 
                 stream(s, z, up_dirs)
             if not last:
-                collide(s + 1, z)
-                if z == planes - 1:
-                    send_up(s + 1)
-                if z == 0:
-                    send_down(s + 1)
+                for c in range(height // chunk):
+                    collide(s + 1, z, c, 1)
+                    if z == planes - 1:
+                        send_up(s + 1, c * chunk, chunk)
+                    if z == 0:
+                        send_down(s + 1, c * chunk, chunk)
                 early(s + 1, z, True)
 
     all_parts().wait_send()

time: 19.2 us -> 18.9 us (0.984)
  Pallas kernels: 17.7 us -> 17.5 us
    pallas_call x1, Pallas kernels: 16.7 us -> 16.4 us  [body(): pl.pallas_call(functools.partial(kernel, n), name='lattice', out_shape=(p...]
where the time goes in v5:
time: 18.9 us; the launch traced here: 18.8 us
  Pallas kernels  17.5 us (93%)
  between operations  1.29 us (7%)
    pallas_call x1, Pallas kernels, body(): pl.pallas_call(functools.partial(kernel, n), name='lattice', out_shape=(p...  16.4 us
    pallas_call x1, Pallas kernels, body(): pl.pallas_call(finish, name='finish', out_shape=(jax.ShapeDtypeStruct(pop...  1.03 us

profile of v5, /device:TPU:1, one launch (start us, length us, event | category | flops | bytes accessed | tf_op | source)
XLA Modules:
  0.0 18.8 jit_solution(14956856912717208273)
XLA Ops:
  1.3 16.4 %lattice.1 = (f32[19,2,64,128]{3,2,1,0:T(8,128)S(1)}, f32[3,2,32]{2,1,0:T(2,128)S(1)}) custom-call(s32[1]{0:T(128)S(6)} %copy.9.frame_ref, f32[19,2,64,128]{3,2,1,0:T(8,128)} %f_hbm.1, s32[2,64,128]{2,1,0:T(8,128)} %solid_hbm.1, s32[2,2,64,128]{3,2,1,0:T(8,128)} %flags_hbm.1, s32[1,512]{1,0:T(1,128)} %bitcast.6, f32[3,32,512]{2,1,0:T(8,128)} %bitcast.4, ...), custom_call_target="tpu_custom_call" | custom-call | tf_op jit(solution)/shard_map/lattice/pallas_call | solution.py:499
  17.7 1.0 %finish.1 = (f32[19,2,64,128]{3,2,1,0:T(8,128)}, f32[3,2,32]{2,1,0:T(2,128)}) custom-call(f32[19,2,64,128]{3,2,1,0:T(8,128)S(1)} %get-tuple-element.6.f_ref, f32[3,2,32]{2,1,0:T(2,128)S(1)} %get-tuple-element.7.inflow_ref), custom_call_target="tpu_custom_call" | custom-call | tf_op jit(solution)/shard_map/finish/pallas_call | solution.py:551

commit v6 on v5

--- a/solution.py
+++ b/solution.py
@@ -459,7 +459,15 @@
                         send_up(s + 1, c * chunk, chunk)
                     if z == 0:
                         send_down(s + 1, c * chunk, chunk)
-                early(s + 1, z, True)
+                if z > 0:
+                    pl.when(me == 0)(functools.partial(early, s + 1, z, True))
+                else:
+                    early(s + 1, 0, True)
+
+                    @pl.when(me > 0)
+                    def _():
+                        for rest in range(1, planes):
+                            early(s + 1, rest, True)
 
     all_parts().wait_send()
 

time: 18.9 us -> 18.9 us (level)
  no operation moved by 1% of the time
where the time goes in v6:
time: 18.9 us; the launch traced here: 18.8 us
  Pallas kernels  17.5 us (93%)
  between operations  1.29 us (7%)
    pallas_call x1, Pallas kernels, body(): pl.pallas_call(functools.partial(kernel, n), name='lattice', out_shape=(p...  16.4 us
    pallas_call x1, Pallas kernels, body(): pl.pallas_call(finish, name='finish', out_shape=(jax.ShapeDtypeStruct(pop...  1.03 us

profile of v6, /device:TPU:1, one launch (start us, length us, event | category | flops | bytes accessed | tf_op | source)
XLA Modules:
  0.0 18.8 jit_solution(5516194634228274632)
XLA Ops:
  1.3 16.4 %lattice.1 = (f32[19,2,64,128]{3,2,1,0:T(8,128)S(1)}, f32[3,2,32]{2,1,0:T(2,128)S(1)}) custom-call(s32[1]{0:T(128)S(6)} %copy.9.frame_ref, f32[19,2,64,128]{3,2,1,0:T(8,128)} %f_hbm.1, s32[2,64,128]{2,1,0:T(8,128)} %solid_hbm.1, s32[2,2,64,128]{3,2,1,0:T(8,128)} %flags_hbm.1, s32[1,512]{1,0:T(1,128)} %bitcast.6, f32[3,32,512]{2,1,0:T(8,128)} %bitcast.4, ...), custom_call_target="tpu_custom_call" | custom-call | tf_op jit(solution)/shard_map/lattice/pallas_call | solution.py:507
  17.7 1.0 %finish.1 = (f32[19,2,64,128]{3,2,1,0:T(8,128)}, f32[3,2,32]{2,1,0:T(2,128)}) custom-call(f32[19,2,64,128]{3,2,1,0:T(8,128)S(1)} %get-tuple-element.6.f_ref, f32[3,2,32]{2,1,0:T(2,128)S(1)} %get-tuple-element.7.inflow_ref), custom_call_target="tpu_custom_call" | custom-call | tf_op jit(solution)/shard_map/finish/pallas_call | solution.py:559
